TPU v7x, 512 devices: a whole 4x8x8 slice. The times are simulated.
512 devices in a mesh: stream: 8 (over y), span: 16 (over z, core), vert: 4 (over x).
Axes of the slice: x: 4, y: 8, z: 8, core: 2. Of those that a mesh axis runs over, the one named last changes fastest.
Arguments:
- fields: float32 [5, 128, 256, 1024], P(None, 'vert', 'span', 'stream'), may hold values from -6 to 6
- solid_frac: float32 [128, 256, 1024], P('vert', 'span', 'stream'), may hold values from 0 to 1
- panels: float32 [32768, 5, 256], P(('stream', 'span', 'vert')), may hold values from -0.015625 to 0.015625
- panel_owner: int32 [32768, 1], P(('stream', 'span', 'vert')), may hold values from 0 to 63; in each aligned block of 64 rows (0 to 63, 64 to 127, ...) at most 2 rows name the same one
- deck_cells: int32 [4, 16, 8, 2048], P('vert', 'span', 'stream'), may hold values from 0 to 65535
- deck_geom: float32 [4, 16, 8, 3, 2048], P('vert', None, 'stream'), may hold values from -6 to 6
- strip_ids: int32 [4, 16, 8, 2048], P('vert', None, 'stream'), may hold values from 0 to 63, as said below
- mode_shapes: float32 [3, 64, 32], replicated, may hold values from -0.0034179688 to 0.0034179688
Outputs:
- new_fields: float32 [5, 128, 256, 1024], P(None, 'vert', 'span', 'stream')
- modal_force: float32 [32], replicated
Inputs may be any that keep to these rules, and one draw needn't show every extreme that they name: `panel_owner`: tile number s * 4 + v for along-deck tile s and vertical tile v. Among the 64 panels of one device no tile is named more than 2 times; some device names some tile exactly 2 times. `strip_ids`: cells of along-deck tile s belong to strips s * 4 to (s + 1) * 4 - 1.
All inputs are finite; a program needn't handle non-finite values.
Results may differ from a plain program's by a relative error of at most 0.00012.
Values sent between devices are 32-bit elements; how exact they have to be, the bound alone decides.
No kernel may reach another device: no remote copies, remote signals or barrier semaphores. Data moves between devices by JAX's collectives and lax.ppermute only.
A program may use at most 128 MiB of HBM per device.

v0:
```python
import math
import jax
import jax.numpy as jnp
from jax import lax
from jax.sharding import PartitionSpec as P

CAP = 2
time_step = 0.15
viscous = 0.05
heat_diff = 0.03
sound_sq = 1.0
buoyant = 0.5
penalty = 0.5
relax_time = 0.5
relax_depth = 8.0
wave_cols = 16


def extended(block, sides, width):
    for axis, dim in sides:
        count = lax.axis_size(axis)
        forward = [(i, i + 1) for i in range(count - 1)]
        backward = [(target, source) for source, target in forward]
        low = lax.ppermute(
            lax.slice_in_dim(block, block.shape[dim] - width, None, axis=dim), axis, forward
        )
        high = lax.ppermute(lax.slice_in_dim(block, 0, width, axis=dim), axis, backward)
        block = jnp.concatenate([low, block, high], axis=dim)
    return block


def wave_basis(heights, widths, total_z, total_y, spec):
    modes = jnp.arange(spec, dtype=jnp.int32)
    across = (modes % wave_cols)[:, None, None]
    upward = (modes // wave_cols)[:, None, None]
    period = total_y * total_z
    phase = (
        across * widths[None, None, :] * total_z + upward * heights[None, :, None] * total_y
    ) % period
    angle = phase.astype(jnp.float32) * (2.0 * math.pi / period)
    return jnp.concatenate([jnp.cos(angle), jnp.sin(angle)], axis=0)


def relax_weights(positions, limit):
    spots = positions.astype(jnp.float32)
    return jnp.where(positions < limit, jnp.exp(-spots / relax_depth) / relax_time, 0.0)


def rates(padded, solid_frac, relax_rate, target_plane):
    centre = padded[:, 1:-1, 1:-1, 1:-1]
    east_side = padded[:, 1:-1, 1:-1, 2:]
    west_side = padded[:, 1:-1, 1:-1, :-2]
    north_side = padded[:, 1:-1, 2:, 1:-1]
    south_side = padded[:, 1:-1, :-2, 1:-1]
    upper_side = padded[:, 2:, 1:-1, 1:-1]
    lower_side = padded[:, :-2, 1:-1, 1:-1]
    grad_x = 0.5 * (east_side - west_side)
    grad_y = 0.5 * (north_side - south_side)
    grad_z = 0.5 * (upper_side - lower_side)
    laplace = (
        east_side + west_side + north_side + south_side + upper_side + lower_side - 6.0 * centre
    )
    speed_x = centre[0]
    speed_y = centre[1]
    speed_z = centre[2]
    carried = speed_x * grad_x + speed_y * grad_y + speed_z * grad_z
    coeffs = jnp.array([viscous, viscous, viscous, viscous, heat_diff], jnp.float32)[
        :, None, None, None
    ]
    damping = solid_frac / penalty
    nudging = relax_rate[None, None, None, :] * (target_plane[:, :, :, None] - centre)
    common = coeffs * laplace - carried + nudging
    extra_terms = jnp.stack(
        [
            -grad_x[3] - damping * speed_x,
            -grad_y[3] - damping * speed_y,
            -grad_z[3] - damping * speed_z + buoyant * centre[4],
            -sound_sq * (grad_x[0] + grad_y[1] + grad_z[2]),
            jnp.zeros_like(speed_x),
        ]
    )
    return common + extra_terms


def pack_slots(flat_panels, target_tile, chosen, tile_count):
    running = jnp.cumsum(chosen, axis=0) - 1
    slot_rank = jnp.sum(chosen * running, axis=1)
    slot_index = target_tile * CAP + slot_rank
    dispatch = (
        slot_index[None, :] == jnp.arange(tile_count * CAP, dtype=jnp.int32)[:, None]
    ).astype(jnp.float32)
    return jnp.dot(dispatch, flat_panels, precision=lax.Precision.HIGHEST)


def strip_forces(traction, labels, strip_count):
    columns = jnp.arange(strip_count, dtype=jnp.int32)

    def add_row(running, item_pair):
        row_values, row_labels = item_pair
        member = (row_labels[:, None] == columns[None, :]).astype(jnp.float32)
        return (running + jnp.dot(row_values, member, precision=lax.Precision.HIGHEST), None)

    start_value = jnp.zeros((traction.shape[1], strip_count), jnp.float32)
    summed, ignored = lax.scan(add_row, start_value, (traction, labels))
    return summed


def on_device(
    fields, solid_frac, panels, panel_owner, deck_cells, deck_geom, strip_ids, mode_shapes
):
    depth_cells = fields.shape[1]
    span_cells = fields.shape[2]
    wind_cells = fields.shape[3]
    n_span = lax.axis_size("span")
    n_vert = lax.axis_size("vert")
    stream_pos = lax.axis_index("stream")
    span_pos = lax.axis_index("span")
    vert_pos = lax.axis_index("vert")
    tile_count = n_span * n_vert
    held_panels = panels.shape[0]
    spec_cols = panels.shape[2]
    flat_panels = panels.reshape(held_panels, 5 * spec_cols)
    target_tile = panel_owner[:, 0]
    chosen = (target_tile[:, None] == jnp.arange(tile_count, dtype=jnp.int32)[None, :]).astype(
        jnp.int32
    )
    outgoing = pack_slots(flat_panels, target_tile, chosen, tile_count)
    arrived = lax.all_to_all(
        outgoing.reshape(tile_count, CAP * 5 * spec_cols),
        ("span", "vert"),
        split_axis=0,
        concat_axis=0,
        tiled=True,
    )
    coeffs = jnp.sum(arrived.reshape(-1, 5 * spec_cols), axis=0)
    coeffs = coeffs.reshape(5, spec_cols)
    heights = vert_pos * depth_cells + jnp.arange(depth_cells, dtype=jnp.int32)
    widths = span_pos * span_cells + jnp.arange(span_cells, dtype=jnp.int32)
    wave_table = wave_basis(
        heights, widths, depth_cells * n_vert, span_cells * n_span, spec_cols // 2
    )
    wave_table = wave_table.reshape(spec_cols, depth_cells * span_cells)
    partial_value = jnp.dot(coeffs, wave_table, precision=lax.Precision.HIGHEST)
    inflow_plane = lax.psum(partial_value, "stream").reshape(5, depth_cells, span_cells)
    target_plane = inflow_plane + jnp.array([1.0, 0.0, 0.0, 0.0, 0.0], jnp.float32)[:, None, None]
    wind_first = stream_pos * wind_cells
    relax_rate = relax_weights(
        wind_first + jnp.arange(wind_cells, dtype=jnp.int32), wind_cells // 2
    )

    def advance(state):
        padded = extended(state, (("stream", 3), ("span", 2), ("vert", 1)), 1)
        return rates(padded, solid_frac, relax_rate, target_plane)

    first_update = fields + time_step * advance(fields)
    second_rate = advance(first_update)
    new_fields = 0.5 * (fields + first_update + time_step * second_rate)
    pressure = new_fields[3].reshape(-1)
    sampled = pressure[deck_cells[0, 0, 0]]
    strip_count = mode_shapes.shape[1]
    rows_all = lax.all_gather(sampled.reshape(1, 1, 1, -1), "span", axis=1, tiled=True)
    traction = rows_all[0, :, 0][:, None, :] * deck_geom[0, :, 0]
    forces = strip_forces(traction, strip_ids[0, :, 0], strip_count)
    modal_part = jnp.einsum("cj,cjm->m", forces, mode_shapes, precision=lax.Precision.HIGHEST)
    modal_force = lax.psum(modal_part, ("stream", "vert"))
    return (new_fields, modal_force)


def solution(mesh):
    return jax.shard_map(
        on_device,
        mesh=mesh,
        in_specs=(
            P(None, "vert", "span", "stream"),
            P("vert", "span", "stream"),
            P(("stream", "span", "vert"), None, None),
            P(("stream", "span", "vert"), None),
            P("vert", "span", "stream", None),
            P("vert", None, "stream", None, None),
            P("vert", None, "stream", None),
            P(),
        ),
        out_specs=(P(None, "vert", "span", "stream"), P()),
        check_vma=False,
    )
```

profile of v0, /device:TPU:64, one launch (start us, length us, event | category | flops | bytes accessed | tf_op | source)
XLA Modules:
  0.0 263.3 jit_solution(5278629360200519969)
XLA Ops:
  0.6 2.2 fusion.52
  5.3 4.5 %collective-permute-start.1 = (f32[5,32,16,1]{1,2,3,0:T(8,128)S(1)}, f32[5,32,16,1]{1,2,3,0:T(8,128)S(1)}, u32[]{:S(2)}, u32[]{:S(2)}) collective-permute-start(f32[5,32,16,1]{1,2,3,0:T(8,128)S(1)} %copy.56), channel_id=1, source_target_pairs={{0,64},{64,128},{128,192},{192,256},{256,320},{320,384},{384,448},... | collective-permute-start | bytes 30728 | tf_op jit(solution)/shard_map/ppermute | solution.py:24
  12.2 13.3 %all-to-all-start = ((f32[64,1,2560]{2,1,0:T(1,128)}), f32[64,1,2560]{2,1,0:T(1,128)}, u32[]{:S(2)}, u32[]{:S(2)}) async-start(f32[64,1,2560]{2,1,0:T(1,128)} %all_to_all.8), calls=%async_computation | async-start | bytes 1310720 | tf_op jit(solution)/shard_map/all_to_all | solution.py:128
  26.7 1.7 fusion.46
  29.1 1.6 copy.39
  30.7 2.5 pad_maximum_fusion.39
  33.2 2.0 collective-permute-start.2
  35.2 2.3 collective-permute-start.3
  37.5 4.0 %collective-permute-done.2 = f32[5,32,1,130]{3,2,1,0:T(1,128)S(1)} collective-permute-done((f32[5,32,1,130]{3,2,1,0:T(1,128)S(1)}, f32[5,32,1,130]{3,2,1,0:T(1,128)S(1)}, u32[]{:S(2)}, u32[]{:S(2)}) %collective-permute-start.2) | collective-permute-done | bytes 83232 | tf_op jit(solution)/shard_map/ppermute | solution.py:27
  41.5 1.5 collective-permute-done.3
  44.5 4.7 %collective-permute-start.5 = (f32[5,1,18,130]{3,2,1,0:T(8,128)S(1)}, f32[5,1,18,130]{3,2,1,0:T(8,128)S(1)}, u32[]{:S(2)}, u32[]{:S(2)}) collective-permute-start(f32[5,1,18,130]{3,2,1,0:T(8,128)S(1)} %get-tuple-element.71), channel_id=1, source_target_pairs={{0,1},{1,2},{2,3},{4,5},{5,6},{6,7},{8,9},{9,10},{10,11},{12,13},{... | collective-permute-start | bytes 140408 | tf_op jit(solution)/shard_map/ppermute | solution.py:24
  51.7 3.2 %broadcast_multiply_fusion.3 = (f32[5,32,16,128]{3,2,1,0:T(8,128)S(1)}, f32[5,32,16,128]{3,2,1,0:T(8,128)S(1)}) fusion(f32[5,1,18,130]{3,2,1,0:T(8,128)S(1)} %collective-permute-done.4, f32[5,32,1,130]{3,2,1,0:T(1,128)S(1)} %collective-permute-done.2, f32[5,32,16,1]{3,2,1,0:T(8,128)S(1)} %copy.37, f32[5,32,16,128]{3,2,1,0:T(8,128)S(1)} %copy-done.1, ...), kind=kLoop, calls=%fused_computation.50 | loop fusion | flops 5242880 | bytes 4212640 | tf_op jit(solution)/shard_map/mul | solution.py:59
  58.7 2.6 %reduce = f32[64,2560]{1,0:T(8,128)S(1)} reduce(f32[64,1,2560]{2,1,0:T(1,128)} %all-to-all-done, f32[]{:T(128)} %constant.123), dimensions={1}, to_apply=%all_to_all.7.reduce_sub_computation | reduce | bytes 1310724 | tf_op jit(solution)/shard_map/all_to_all | solution.py:128
  63.1 30.8 %psum.14 = f32[5,32,16]{2,1,0:T(8,128)S(1)} all-reduce(f32[5,32,16]{2,1,0:T(8,128)S(1)} %reshape.200), channel_id=1, replica_groups=mesh['stream'=8,'span'=16,'vert'=4] {'stream'}, use_global_device_ids=true, to_apply=%region_3.4 | all-reduce | flops 2560 | bytes 20480 | tf_op jit(solution)/shard_map/psum | solution.py:144
  94.0 7.5 %multiply_add_fusion = f32[5,32,16,128]{3,2,1,0:T(8,128)S(1)} fusion(f32[5,32,16,128]{3,2,1,0:T(8,128)S(1)} %copy-done.1, f32[5,32,16,128]{3,2,1,0:T(8,128)} %broadcast_dynamic-update-slice_fusion.1, f32[5,32,16]{2,1,0:T(8,128)S(1)} %broadcast_add_fusion.1, f32[128]{0:T(128)S(1)} %compare_select_fusion.1, f32[32,16,128]{2,1,0:T(8,128)} %get-tuple-element.87, ...), kind=kLoop, calls=%fused_computation.45 | loop fusion | flops 13434880 | bytes 5009844 | tf_op jit(solution)/shard_map/add | solution.py:155
  101.5 1.9 fusion.51
  103.5 1.9 copy.44
  106.7 1.9 copy.46
  108.5 4.5 %collective-permute-start.7 = (f32[5,32,16,1]{1,2,3,0:T(8,128)S(1)}, f32[5,32,16,1]{1,2,3,0:T(8,128)S(1)}, u32[]{:S(2)}, u32[]{:S(2)}) collective-permute-start(f32[5,32,16,1]{1,2,3,0:T(8,128)S(1)} %copy.46), channel_id=1, source_target_pairs={{0,64},{64,128},{128,192},{192,256},{256,320},{320,384},{384,448},... | collective-permute-start | bytes 30728 | tf_op jit(solution)/shard_map/ppermute | solution.py:24
  113.2 1.6 copy.45
  114.8 1.6 copy.47
  116.4 2.9 %pad_maximum_fusion.36 = (f32[5,32,1,130]{3,2,1,0:T(1,128)S(1)}, f32[5,32,1,130]{3,2,1,0:T(1,128)S(1)}) fusion(f32[5,32,16,1]{3,2,1,0:T(8,128)} %copy.45, f32[5,32,16,128]{3,2,1,0:T(8,128)S(1)} %multiply_add_fusion, f32[5,32,16,1]{3,2,1,0:T(8,128)} %copy.47), kind=kLoop, calls=%fused_computation.118 | loop fusion | flops 83200 | bytes 1497600 | tf_op jit(solution)/shard_map/concatenate | solution.py:28
  119.3 2.1 collective-permute-start.8
  121.4 2.6 collective-permute-start.9
  124.2 3.8 %collective-permute-done.9 = f32[5,32,1,130]{3,2,1,0:T(1,128)S(1)} collective-permute-done((f32[5,32,1,130]{3,2,1,0:T(1,128)S(1)}, f32[5,32,1,130]{3,2,1,0:T(1,128)S(1)}, u32[]{:S(2)}, u32[]{:S(2)}) %collective-permute-start.9) | collective-permute-done | bytes 83232 | tf_op jit(solution)/shard_map/ppermute | solution.py:24
  129.5 5.0 %collective-permute-start.11 = (f32[5,1,18,130]{3,2,1,0:T(8,128)S(1)}, f32[5,1,18,130]{3,2,1,0:T(8,128)S(1)}, u32[]{:S(2)}, u32[]{:S(2)}) collective-permute-start(f32[5,1,18,130]{3,2,1,0:T(8,128)S(1)} %get-tuple-element.69), channel_id=1, source_target_pairs={{0,1},{1,2},{2,3},{4,5},{5,6},{6,7},{8,9},{9,10},{10,11},{12,13},{... | collective-permute-start | bytes 140408 | tf_op jit(solution)/shard_map/ppermute | solution.py:24
  136.9 3.1 %broadcast_multiply_fusion = (f32[5,32,16,128]{3,2,1,0:T(8,128)S(1)}, f32[5,32,16,128]{3,2,1,0:T(8,128)S(1)}) fusion(f32[5,1,18,130]{3,2,1,0:T(8,128)S(1)} %collective-permute-done.10, f32[5,32,1,130]{3,2,1,0:T(1,128)S(1)} %collective-permute-done.8, f32[5,32,16,1]{3,2,1,0:T(8,128)S(1)} %copy-done.4, f32[5,32,16,128]{3,2,1,0:T(8,128)S(1)} %multiply_add_fusion, ...), kind=kLoop, calls=%fused_computation.47 | loop fusion | flops 5242880 | bytes 4212640 | tf_op jit(solution)/shard_map/mul | solution.py:59
  140.4 5.0 %add_multiply_fusion = f32[5,32,16,128]{3,2,1,0:T(8,128)S(1)} fusion(f32[5,32,16,128]{3,2,1,0:T(8,128)S(1)} %broadcast_dynamic-update-slice_fusion, f32[5,32,16,128]{3,2,1,0:T(8,128)S(1)} %multiply_add_fusion, f32[5,32,16,128]{3,2,1,0:T(8,128)S(1)} %copy-done.1, f32[32,16,128]{2,1,0:T(8,128)S(1)} %get-tuple-element.82, ...), kind=kLoop, calls=%fused_computation.44 | loop fusion | flops 14090240 | bytes 6320564 | tf_op jit(solution)/shard_map/mul | solution.py:157
  146.5 11.8 %gather_fusion = f32[2048]{0:T(1024)S(1)} fusion(f32[65536]{0:T(1024)S(1)} %bitcast.150, s32[2048]{0:T(1024)S(1)} %broadcast_clamp_fusion), kind=kCustom, calls=%fused_computation | custom fusion | bytes 24576 | tf_op jit(solution)/shard_map/gather | solution.py:159
  158.2 16.8 %all-gather = f32[32768]{0:T(1024)S(1)} all-gather(f32[2048]{0:T(1024)S(1)} %gather_fusion), channel_id=2, replica_groups=mesh['stream'=8,'span'=16,'vert'=4] {'span'}, dimensions={0}, use_global_device_ids=true | all-gather | bytes 139264 | tf_op jit(solution)/shard_map/all_gather | solution.py:161
  175.2 10.6 %while.11 = (s32[]{:T(128)}, f32[3,64]{1,0:T(4,128)S(1)}, f32[16,3,2048]{2,0,1:T(8,128)S(1)}, s32[16,2048]{1,0:T(8,128)S(1)}, s32[]{:T(128)}, /*index=5*/s32[]{:T(128)}) while((s32[]{:T(128)}, f32[3,64]{1,0:T(4,128)S(1)}, f32[16,3,2048]{2,0,1:T(8,128)S(1)}, s32[16,2048]{1,0:T(8,128)S(1)}, s32[]{:T(128)}, /*index=5*/s32[]{:T(128)}) %tuple.46), condition=%wide.region_5.6_spmd.clone, body=%wide.region_4.5_spmd.clone.sunk | while | flops 4850051 | bytes 99927 | solution.py:104
  186.0 77.3 %psum.15 = f32[32]{0:T(128)} all-reduce(f32[32]{0:T(128)S(1)} %convolution_bitcast_fusion), channel_id=1, replica_groups=mesh['stream'=8,'span'=16,'vert'=4] {'stream','vert'}, use_global_device_ids=true, to_apply=%region_6.7 | all-reduce | flops 32 | bytes 256 | tf_op jit(solution)/shard_map/psum | solution.py:165
  (144 shorter events, 33.0 us)
Async XLA Ops:
  0.6 185.2 %copy-start = (f32[3,64,32]{1,2,0:T(8,128)S(1)}, f32[3,64,32]{1,2,0:T(8,128)}, u32[]{:S(2)}) copy-start(f32[3,64,32]{1,2,0:T(8,128)} %param.20) | copy-start | bytes 73732
  2.8 7.1 %copy-start.14 = (s32[64,1]{0,1:T(1,128)S(1)}, s32[64,1]{0,1:T(1,128)}, u32[]{:S(2)}) copy-start(s32[64,1]{0,1:T(1,128)} %param.16) | copy-start | bytes 772
  2.8 7.4 %copy-start.11 = (f32[64,5,256]{2,0,1:T(8,128)S(1)}, f32[64,5,256]{2,0,1:T(8,128)}, u32[]{:S(2)}) copy-start(f32[64,5,256]{2,0,1:T(8,128)} %param.15) | copy-start | bytes 983044
  3.4 25.0 %collective-permute-start = (f32[5,32,16,1]{1,2,3,0:T(8,128)S(1)}, f32[5,32,16,1]{1,2,3,0:T(8,128)S(1)}, u32[]{:S(2)}, u32[]{:S(2)}) collective-permute-start(f32[5,32,16,1]{1,2,3,0:T(8,128)S(1)} %copy.55), channel_id=1, source_target_pairs={{64,0},{128,64},{192,128},{256,192},{320,256},{384,320},{448,384},... | collective-permute-start | bytes 30728 | tf_op jit(solution)/shard_map/ppermute | solution.py:27
  5.3 23.7 %collective-permute-start.1 = (f32[5,32,16,1]{1,2,3,0:T(8,128)S(1)}, f32[5,32,16,1]{1,2,3,0:T(8,128)S(1)}, u32[]{:S(2)}, u32[]{:S(2)}) collective-permute-start(f32[5,32,16,1]{1,2,3,0:T(8,128)S(1)} %copy.56), channel_id=1, source_target_pairs={{0,64},{64,128},{128,192},{192,256},{256,320},{320,384},{384,448},... | collective-permute-start | bytes 30728 | tf_op jit(solution)/shard_map/ppermute | solution.py:24
  10.7 14.8 %copy-start.1 = (f32[5,32,16,128]{3,2,1,0:T(8,128)S(1)}, f32[5,32,16,128]{3,2,1,0:T(8,128)}, u32[]{:S(2)}) copy-start(f32[5,32,16,128]{3,2,1,0:T(8,128)} %param.13) | copy-start | bytes 3932164
  12.2 14.2 %copy-start.13 = (s32[1,1,1,2048]{3,2,1,0:T(1,128)S(1)}, s32[1,1,1,2048]{3,2,1,0:T(1,128)}, u32[]{:S(2)}) copy-start(s32[1,1,1,2048]{3,2,1,0:T(1,128)} %param.17) | copy-start | bytes 24580
  12.2 46.5 %all-to-all-start = ((f32[64,1,2560]{2,1,0:T(1,128)}), f32[64,1,2560]{2,1,0:T(1,128)}, u32[]{:S(2)}, u32[]{:S(2)}) async-start(f32[64,1,2560]{2,1,0:T(1,128)} %all_to_all.8), calls=%async_computation | async-start | bytes 1310720 | tf_op jit(solution)/shard_map/all_to_all | solution.py:128
  29.1 22.7 %copy-start.2 = (f32[5,32,16,1]{3,2,1,0:T(8,128)}, f32[5,32,16,1]{3,2,1,0:T(8,128)S(1)}, u32[]{:S(2)}) copy-start(f32[5,32,16,1]{3,2,1,0:T(8,128)S(1)} %copy.37) | copy-start | bytes 30724
  30.7 12.4 %copy-start.3 = (f32[5,32,16,1]{3,2,1,0:T(8,128)S(1)}, f32[5,32,16,1]{3,2,1,0:T(8,128)}, u32[]{:S(2)}) copy-start(f32[5,32,16,1]{3,2,1,0:T(8,128)} %copy.39) | copy-start | bytes 30724
  33.2 8.4 %collective-permute-start.2 = (f32[5,32,1,130]{3,2,1,0:T(1,128)S(1)}, f32[5,32,1,130]{3,2,1,0:T(1,128)S(1)}, u32[]{:S(2)}, u32[]{:S(2)}) collective-permute-start(f32[5,32,1,130]{3,2,1,0:T(1,128)S(1)} %get-tuple-element.80), channel_id=1, source_target_pairs={{4,0},{8,4},{12,8},{16,12},{20,16},{24,20},{28,24},{32,28},{36,32}... | collective-permute-start | bytes 249608 | tf_op jit(solution)/shard_map/ppermute | solution.py:27
  35.2 7.9 %collective-permute-start.3 = (f32[5,32,1,130]{3,2,1,0:T(1,128)S(1)}, f32[5,32,1,130]{3,2,1,0:T(1,128)S(1)}, u32[]{:S(2)}, u32[]{:S(2)}) collective-permute-start(f32[5,32,1,130]{3,2,1,0:T(1,128)S(1)} %get-tuple-element.79), channel_id=1, source_target_pairs={{0,4},{4,8},{8,12},{12,16},{16,20},{20,24},{24,28},{28,32},{32,36}... | collective-permute-start | bytes 249608 | tf_op jit(solution)/shard_map/ppermute | solution.py:24
  43.2 7.3 %collective-permute-start.4 = (f32[5,1,18,130]{3,2,1,0:T(8,128)S(1)}, f32[5,1,18,130]{3,2,1,0:T(8,128)S(1)}, u32[]{:S(2)}, u32[]{:S(2)}) collective-permute-start(f32[5,1,18,130]{3,2,1,0:T(8,128)S(1)} %get-tuple-element.72), channel_id=1, source_target_pairs={{1,0},{2,1},{3,2},{5,4},{6,5},{7,6},{9,8},{10,9},{11,10},{13,12},{... | collective-permute-start | bytes 140408 | tf_op jit(solution)/shard_map/ppermute | solution.py:27
  44.5 7.2 %collective-permute-start.5 = (f32[5,1,18,130]{3,2,1,0:T(8,128)S(1)}, f32[5,1,18,130]{3,2,1,0:T(8,128)S(1)}, u32[]{:S(2)}, u32[]{:S(2)}) collective-permute-start(f32[5,1,18,130]{3,2,1,0:T(8,128)S(1)} %get-tuple-element.71), channel_id=1, source_target_pairs={{0,1},{1,2},{2,3},{4,5},{5,6},{6,7},{8,9},{9,10},{10,11},{12,13},{... | collective-permute-start | bytes 140408 | tf_op jit(solution)/shard_map/ppermute | solution.py:24
  50.4 4.5 %copy-start.6 = (f32[32,16,128]{2,1,0:T(8,128)S(1)}, f32[32,16,128]{2,1,0:T(8,128)}, u32[]{:S(2)}) copy-start(f32[32,16,128]{2,1,0:T(8,128)} %param.14) | copy-start | bytes 786436
  50.5 4.4 %copy-start.8 = (f32[5,1,18,130]{3,2,1,0:T(8,128)}, f32[5,1,18,130]{3,2,1,0:T(8,128)S(1)}, u32[]{:S(2)}) copy-start(f32[5,1,18,130]{3,2,1,0:T(8,128)S(1)} %collective-permute-done.4) | copy-start | bytes 140404
  51.7 3.2 %copy-start.9 = (f32[5,1,18,130]{3,2,1,0:T(8,128)}, f32[5,1,18,130]{3,2,1,0:T(8,128)S(1)}, u32[]{:S(2)}) copy-start(f32[5,1,18,130]{3,2,1,0:T(8,128)S(1)} %collective-permute-done.5) | copy-start | bytes 140404
  61.3 32.6 %copy-start.16 = (f32[5]{0:T(128)S(1)}, f32[5]{0:T(128)}, u32[]{:S(2)}) copy-start(f32[5]{0:T(128)} %constant.116.clone) | copy-start | bytes 64
  61.4 32.6 %copy-start.15 = (f32[5]{0:T(128)S(1)}, f32[5]{0:T(128)}, u32[]{:S(2)}) copy-start(f32[5]{0:T(128)} %constant.117.clone) | copy-start | bytes 64
  103.5 9.7 %copy-start.12 = (s32[1,16,1,2048]{3,2,1,0:T(1,128)S(1)}, s32[1,16,1,2048]{3,2,1,0:T(1,128)}, u32[]{:S(2)}) copy-start(s32[1,16,1,2048]{3,2,1,0:T(1,128)} %param.19) | copy-start | bytes 393220
  105.4 7.8 %collective-permute-start.6 = (f32[5,32,16,1]{1,2,3,0:T(8,128)S(1)}, f32[5,32,16,1]{1,2,3,0:T(8,128)S(1)}, u32[]{:S(2)}, u32[]{:S(2)}) collective-permute-start(f32[5,32,16,1]{1,2,3,0:T(8,128)S(1)} %copy.44), channel_id=1, source_target_pairs={{64,0},{128,64},{192,128},{256,192},{320,256},{384,320},{448,384},... | collective-permute-start | bytes 30728 | tf_op jit(solution)/shard_map/ppermute | solution.py:27
  108.5 6.3 %collective-permute-start.7 = (f32[5,32,16,1]{1,2,3,0:T(8,128)S(1)}, f32[5,32,16,1]{1,2,3,0:T(8,128)S(1)}, u32[]{:S(2)}, u32[]{:S(2)}) collective-permute-start(f32[5,32,16,1]{1,2,3,0:T(8,128)S(1)} %copy.46), channel_id=1, source_target_pairs={{0,64},{64,128},{128,192},{192,256},{256,320},{320,384},{384,448},... | collective-permute-start | bytes 30728 | tf_op jit(solution)/shard_map/ppermute | solution.py:24
  116.4 11.6 %copy-start.5 = (f32[5,32,16,1]{3,2,1,0:T(8,128)S(1)}, f32[5,32,16,1]{3,2,1,0:T(8,128)}, u32[]{:S(2)}) copy-start(f32[5,32,16,1]{3,2,1,0:T(8,128)} %copy.47) | copy-start | bytes 30724
  119.3 8.7 %copy-start.4 = (f32[5,32,16,1]{3,2,1,0:T(8,128)S(1)}, f32[5,32,16,1]{3,2,1,0:T(8,128)}, u32[]{:S(2)}) copy-start(f32[5,32,16,1]{3,2,1,0:T(8,128)} %copy.45) | copy-start | bytes 30724
  119.3 4.9 %collective-permute-start.8 = (f32[5,32,1,130]{3,2,1,0:T(1,128)S(1)}, f32[5,32,1,130]{3,2,1,0:T(1,128)S(1)}, u32[]{:S(2)}, u32[]{:S(2)}) collective-permute-start(f32[5,32,1,130]{3,2,1,0:T(1,128)S(1)} %get-tuple-element.76), channel_id=1, source_target_pairs={{4,0},{8,4},{12,8},{16,12},{20,16},{24,20},{28,24},{32,28},{36,32}... | collective-permute-start | bytes 249608 | tf_op jit(solution)/shard_map/ppermute | solution.py:27
  121.4 6.6 %collective-permute-start.9 = (f32[5,32,1,130]{3,2,1,0:T(1,128)S(1)}, f32[5,32,1,130]{3,2,1,0:T(1,128)S(1)}, u32[]{:S(2)}, u32[]{:S(2)}) collective-permute-start(f32[5,32,1,130]{3,2,1,0:T(1,128)S(1)} %get-tuple-element.75), channel_id=1, source_target_pairs={{0,4},{4,8},{8,12},{12,16},{16,20},{20,24},{24,28},{28,32},{32,36}... | collective-permute-start | bytes 249608 | tf_op jit(solution)/shard_map/ppermute | solution.py:24
  128.2 7.4 %collective-permute-start.10 = (f32[5,1,18,130]{3,2,1,0:T(8,128)S(1)}, f32[5,1,18,130]{3,2,1,0:T(8,128)S(1)}, u32[]{:S(2)}, u32[]{:S(2)}) collective-permute-start(f32[5,1,18,130]{3,2,1,0:T(8,128)S(1)} %get-tuple-element.70), channel_id=1, source_target_pairs={{1,0},{2,1},{3,2},{5,4},{6,5},{7,6},{9,8},{10,9},{11,10},{13,12},{... | collective-permute-start | bytes 140408 | tf_op jit(solution)/shard_map/ppermute | solution.py:27
  129.5 7.4 %collective-permute-start.11 = (f32[5,1,18,130]{3,2,1,0:T(8,128)S(1)}, f32[5,1,18,130]{3,2,1,0:T(8,128)S(1)}, u32[]{:S(2)}, u32[]{:S(2)}) collective-permute-start(f32[5,1,18,130]{3,2,1,0:T(8,128)S(1)} %get-tuple-element.69), channel_id=1, source_target_pairs={{0,1},{1,2},{2,3},{4,5},{5,6},{6,7},{8,9},{9,10},{10,11},{12,13},{... | collective-permute-start | bytes 140408 | tf_op jit(solution)/shard_map/ppermute | solution.py:24
  145.4 1.1 copy-start.7
  146.4 28.6 %copy-start.10 = (f32[1,16,1,3,2048]{4,2,3,1,0:T(1,128)S(1)}, f32[1,16,1,3,2048]{4,2,3,1,0:T(1,128)}, u32[]{:S(2)}) copy-start(f32[1,16,1,3,2048]{4,2,3,1,0:T(1,128)} %param.18) | copy-start | bytes 1179652
where the time goes:
time: 264 us; the launch traced here: 263 us
  blocking collectives  125 us (47%)
  starting transfers between devices  46.3 us (18%)
  other arithmetic  36.1 us (14%)
  local copies, waits for them, and re-layouts  30.7 us (12%)
  waiting for transfers between devices  12.1 us (5%)
  matrix products  11.3 us (4%)
    psum x1, blocking collectives, on_device(): modal_force = lax.psum(modal_part, ('stream', 'vert'))  77.3 us
    psum x1, blocking collectives, on_device(): lax.psum(partial_value, 'stream').reshape(5, depth_cells, span_cells)  30.8 us
    ppermute x6, starting transfers between devices, extended(): lax.ppermute(lax.slice_in_dim(block, block.shape[dim] - width, None, axis...  23.8 us
    all_gather x1, blocking collectives, on_device(): lax.all_gather(sampled.reshape(1, 1, 1, -1), 'span', axis=1, tiled=True)  16.8 us
    all_to_all x1, starting transfers between devices, on_device(): lax.all_to_all(outgoing.reshape(tile_count, CAP * 5 * spec_cols), ('span'...  13.3 us
    gather x1, local copies, waits for them, and re-layouts, on_device(): sampled = pressure[deck_cells[0, 0, 0]]  11.8 us
    dot_general x16, matrix products, add_row(): jnp.dot(row_values, member, precision=lax.Precision.HIGHEST)  9.31 us
    ppermute x6, starting transfers between devices, extended(): lax.ppermute(lax.slice_in_dim(block, 0, width, axis=dim), axis, backward)  9.23 us
  transfers between devices with their start and end apart: 13, of which 7 were waited for; matrix products, arithmetic and copies ran while one was open for 8% of the time, Pallas kernels for 0%

commit v1 on v0

--- a/solution.py
+++ b/solution.py
@@ -141,7 +141,9 @@
     )
     wave_table = wave_table.reshape(spec_cols, depth_cells * span_cells)
     partial_value = jnp.dot(coeffs, wave_table, precision=lax.Precision.HIGHEST)
-    inflow_plane = lax.psum(partial_value, "stream").reshape(5, depth_cells, span_cells)
+    inflow_plane = jnp.sum(lax.all_gather(partial_value, "stream"), axis=0).reshape(
+        5, depth_cells, span_cells
+    )
     target_plane = inflow_plane + jnp.array([1.0, 0.0, 0.0, 0.0, 0.0], jnp.float32)[:, None, None]
     wind_first = stream_pos * wind_cells
     relax_rate = relax_weights(

time: 264 us -> 260 us (0.985)
  the two profiles are of different devices: /device:TPU:64 before, /device:TPU:32 now
where the time goes in v1:
time: 260 us; the launch traced here: 259 us
  blocking collectives  124 us (48%)
  starting transfers between devices  47.1 us (18%)
  other arithmetic  36.1 us (14%)
  local copies, waits for them, and re-layouts  30.7 us (12%)
  matrix products  11.3 us (4%)
  waiting for transfers between devices  7.42 us (3%)
    psum x1, blocking collectives, on_device(): modal_force = lax.psum(modal_part, ('stream', 'vert'))  73.9 us
    all_gather x1, blocking collectives, on_device(): lax.all_gather(sampled.reshape(1, 1, 1, -1), 'span', axis=1, tiled=True)  25.7 us
    all_gather x1, blocking collectives, on_device(): lax.all_gather(partial_value, 'stream')  24.6 us
    ppermute x6, starting transfers between devices, extended(): lax.ppermute(lax.slice_in_dim(block, block.shape[dim] - width, None, axis...  21.5 us
    all_to_all x1, starting transfers between devices, on_device(): lax.all_to_all(outgoing.reshape(tile_count, CAP * 5 * spec_cols), ('span'...  14.1 us
    gather x1, local copies, waits for them, and re-layouts, on_device(): sampled = pressure[deck_cells[0, 0, 0]]  11.8 us
    ppermute x6, starting transfers between devices, extended(): lax.ppermute(lax.slice_in_dim(block, 0, width, axis=dim), axis, backward)  11.4 us
    dot_general x16, matrix products, add_row(): jnp.dot(row_values, member, precision=lax.Precision.HIGHEST)  9.31 us
  transfers between devices with their start and end apart: 13, of which 5 were waited for; matrix products, arithmetic and copies ran while one was open for 8% of the time, Pallas kernels for 0%

profile of v1, /device:TPU:32, one launch (start us, length us, event | category | flops | bytes accessed | tf_op | source)
XLA Modules:
  0.0 258.8 jit_solution(14789413413344441210)
XLA Ops:
  0.6 2.2 fusion.51
  3.4 2.4 collective-permute-start
  6.4 3.5 %collective-permute-start.1 = (f32[5,32,16,1]{1,2,3,0:T(8,128)S(1)}, f32[5,32,16,1]{1,2,3,0:T(8,128)S(1)}, u32[]{:S(2)}, u32[]{:S(2)}) collective-permute-start(f32[5,32,16,1]{1,2,3,0:T(8,128)S(1)} %copy.56), channel_id=1, source_target_pairs={{0,64},{64,128},{128,192},{192,256},{256,320},{320,384},{384,448},... | collective-permute-start | bytes 30728 | tf_op jit(solution)/shard_map/ppermute | solution.py:24
  10.7 1.5 all_to_all.8
  12.2 14.1 %all-to-all-start = ((f32[64,1,2560]{2,1,0:T(1,128)}), f32[64,1,2560]{2,1,0:T(1,128)}, u32[]{:S(2)}, u32[]{:S(2)}) async-start(f32[64,1,2560]{2,1,0:T(1,128)} %all_to_all.8), calls=%async_computation | async-start | bytes 1310720 | tf_op jit(solution)/shard_map/all_to_all | solution.py:128
  27.5 1.7 fusion.45
  29.9 1.6 copy.39
  31.6 2.5 pad_maximum_fusion.39
  35.3 3.0 %collective-permute-start.3 = (f32[5,32,1,130]{3,2,1,0:T(1,128)S(1)}, f32[5,32,1,130]{3,2,1,0:T(1,128)S(1)}, u32[]{:S(2)}, u32[]{:S(2)}) collective-permute-start(f32[5,32,1,130]{3,2,1,0:T(1,128)S(1)} %get-tuple-element.79), channel_id=1, source_target_pairs={{0,4},{4,8},{8,12},{12,16},{16,20},{20,24},{24,28},{28,32},{32,36}... | collective-permute-start | bytes 249608 | tf_op jit(solution)/shard_map/ppermute | solution.py:24
  40.9 4.7 %collective-permute-start.5 = (f32[5,1,18,130]{3,2,1,0:T(8,128)S(1)}, f32[5,1,18,130]{3,2,1,0:T(8,128)S(1)}, u32[]{:S(2)}, u32[]{:S(2)}) collective-permute-start(f32[5,1,18,130]{3,2,1,0:T(8,128)S(1)} %get-tuple-element.71), channel_id=1, source_target_pairs={{0,1},{1,2},{2,3},{4,5},{5,6},{6,7},{8,9},{9,10},{10,11},{12,13},{... | collective-permute-start | bytes 140408 | tf_op jit(solution)/shard_map/ppermute | solution.py:24
  47.8 3.2 %broadcast_multiply_fusion.3 = (f32[5,32,16,128]{3,2,1,0:T(8,128)S(1)}, f32[5,32,16,128]{3,2,1,0:T(8,128)S(1)}) fusion(f32[5,1,18,130]{3,2,1,0:T(8,128)S(1)} %collective-permute-done.4, f32[5,32,1,130]{3,2,1,0:T(1,128)S(1)} %collective-permute-done.2, f32[5,32,16,1]{3,2,1,0:T(8,128)S(1)} %copy.37, f32[5,32,16,128]{3,2,1,0:T(8,128)S(1)} %copy-done.1, ...), kind=kLoop, calls=%fused_computation.51 | loop fusion | flops 5242880 | bytes 4212640 | tf_op jit(solution)/shard_map/mul | solution.py:59
  54.8 2.6 %reduce.1 = f32[64,2560]{1,0:T(8,128)S(1)} reduce(f32[64,1,2560]{2,1,0:T(1,128)} %all-to-all-done, f32[]{:T(128)} %constant.123), dimensions={1}, to_apply=%all_to_all.7.reduce_sub_computation | reduce | bytes 1310724 | tf_op jit(solution)/shard_map/all_to_all | solution.py:128
  59.1 24.6 %all-gather.2 = f32[8,5,512]{2,1,0:T(8,128)S(1)} all-gather(f32[1,5,512]{2,1,0:T(8,128)S(1)} %convolution_bitcast_fusion), channel_id=2, replica_groups=mesh['stream'=8,'span'=16,'vert'=4] {'stream'}, dimensions={0}, use_global_device_ids=true | all-gather | bytes 92160 | tf_op jit(solution)/shard_map/all_gather | solution.py:144
  84.0 7.5 %multiply_add_fusion = f32[5,32,16,128]{3,2,1,0:T(8,128)S(1)} fusion(f32[5,32,16,128]{3,2,1,0:T(8,128)S(1)} %copy-done.1, f32[5,32,16,128]{3,2,1,0:T(8,128)} %broadcast_dynamic-update-slice_fusion.1, f32[5,32,16]{2,1,0:T(8,128)S(1)} %broadcast_add_fusion.1, f32[128]{0:T(128)S(1)} %compare_select_fusion.1, f32[32,16,128]{2,1,0:T(8,128)} %get-tuple-element.87, ...), kind=kLoop, calls=%fused_computation.45 | loop fusion | flops 13434880 | bytes 5009844 | tf_op jit(solution)/shard_map/add | solution.py:157
  91.5 1.9 fusion.50
  93.4 1.9 copy.44
  95.3 3.5 %collective-permute-start.6 = (f32[5,32,16,1]{1,2,3,0:T(8,128)S(1)}, f32[5,32,16,1]{1,2,3,0:T(8,128)S(1)}, u32[]{:S(2)}, u32[]{:S(2)}) collective-permute-start(f32[5,32,16,1]{1,2,3,0:T(8,128)S(1)} %copy.44), channel_id=1, source_target_pairs={{64,0},{128,64},{192,128},{256,192},{320,256},{384,320},{448,384},... | collective-permute-start | bytes 30728 | tf_op jit(solution)/shard_map/ppermute | solution.py:27
  98.9 1.9 copy.46
  100.8 2.3 collective-permute-start.7
  103.1 1.6 copy.45
  104.8 3.1 %collective-permute-done.7 = f32[5,32,16,1]{1,2,3,0:T(8,128)S(1)} collective-permute-done((f32[5,32,16,1]{1,2,3,0:T(8,128)S(1)}, f32[5,32,16,1]{1,2,3,0:T(8,128)S(1)}, u32[]{:S(2)}, u32[]{:S(2)}) %collective-permute-start.7) | collective-permute-done | bytes 10272 | tf_op jit(solution)/shard_map/ppermute | solution.py:24
  107.9 1.6 copy.47
  109.5 2.9 %pad_maximum_fusion.36 = (f32[5,32,1,130]{3,2,1,0:T(1,128)S(1)}, f32[5,32,1,130]{3,2,1,0:T(1,128)S(1)}) fusion(f32[5,32,16,1]{3,2,1,0:T(8,128)} %copy.45, f32[5,32,16,128]{3,2,1,0:T(8,128)S(1)} %multiply_add_fusion, f32[5,32,16,1]{3,2,1,0:T(8,128)} %copy.47), kind=kLoop, calls=%fused_computation.118 | loop fusion | flops 83200 | bytes 1497600 | tf_op jit(solution)/shard_map/concatenate | solution.py:28
  113.8 3.0 %collective-permute-start.9 = (f32[5,32,1,130]{3,2,1,0:T(1,128)S(1)}, f32[5,32,1,130]{3,2,1,0:T(1,128)S(1)}, u32[]{:S(2)}, u32[]{:S(2)}) collective-permute-start(f32[5,32,1,130]{3,2,1,0:T(1,128)S(1)} %get-tuple-element.75), channel_id=1, source_target_pairs={{0,4},{4,8},{8,12},{12,16},{16,20},{20,24},{24,28},{28,32},{32,36}... | collective-permute-start | bytes 249608 | tf_op jit(solution)/shard_map/ppermute | solution.py:24
  118.0 1.5 collective-permute-start.10
  119.5 4.9 %collective-permute-start.11 = (f32[5,1,18,130]{3,2,1,0:T(8,128)S(1)}, f32[5,1,18,130]{3,2,1,0:T(8,128)S(1)}, u32[]{:S(2)}, u32[]{:S(2)}) collective-permute-start(f32[5,1,18,130]{3,2,1,0:T(8,128)S(1)} %get-tuple-element.69), channel_id=1, source_target_pairs={{0,1},{1,2},{2,3},{4,5},{5,6},{6,7},{8,9},{9,10},{10,11},{12,13},{... | collective-permute-start | bytes 140408 | tf_op jit(solution)/shard_map/ppermute | solution.py:24
  126.9 3.1 %broadcast_multiply_fusion = (f32[5,32,16,128]{3,2,1,0:T(8,128)S(1)}, f32[5,32,16,128]{3,2,1,0:T(8,128)S(1)}) fusion(f32[5,1,18,130]{3,2,1,0:T(8,128)S(1)} %collective-permute-done.10, f32[5,32,1,130]{3,2,1,0:T(1,128)S(1)} %collective-permute-done.8, f32[5,32,16,1]{3,2,1,0:T(8,128)S(1)} %copy-done.4, f32[5,32,16,128]{3,2,1,0:T(8,128)S(1)} %multiply_add_fusion, ...), kind=kLoop, calls=%fused_computation.48 | loop fusion | flops 5242880 | bytes 4212640 | tf_op jit(solution)/shard_map/mul | solution.py:59
  130.3 5.0 %add_multiply_fusion = f32[5,32,16,128]{3,2,1,0:T(8,128)S(1)} fusion(f32[5,32,16,128]{3,2,1,0:T(8,128)S(1)} %broadcast_dynamic-update-slice_fusion, f32[5,32,16,128]{3,2,1,0:T(8,128)S(1)} %multiply_add_fusion, f32[5,32,16,128]{3,2,1,0:T(8,128)S(1)} %copy-done.1, f32[32,16,128]{2,1,0:T(8,128)S(1)} %get-tuple-element.82, ...), kind=kLoop, calls=%fused_computation.44 | loop fusion | flops 14090240 | bytes 6320564 | tf_op jit(solution)/shard_map/mul | solution.py:159
  136.4 11.8 %gather_fusion = f32[2048]{0:T(1024)S(1)} fusion(f32[65536]{0:T(1024)S(1)} %bitcast.152, s32[2048]{0:T(1024)S(1)} %broadcast_clamp_fusion), kind=kCustom, calls=%fused_computation | custom fusion | bytes 24576 | tf_op jit(solution)/shard_map/gather | solution.py:161
  148.2 25.7 %all-gather.1 = f32[32768]{0:T(1024)S(1)} all-gather(f32[2048]{0:T(1024)S(1)} %gather_fusion), channel_id=3, replica_groups=mesh['stream'=8,'span'=16,'vert'=4] {'span'}, dimensions={0}, use_global_device_ids=true | all-gather | bytes 139264 | tf_op jit(solution)/shard_map/all_gather | solution.py:163
  174.1 10.6 %while.11 = (s32[]{:T(128)}, f32[3,64]{1,0:T(4,128)S(1)}, f32[16,3,2048]{2,0,1:T(8,128)S(1)}, s32[16,2048]{1,0:T(8,128)S(1)}, s32[]{:T(128)}, /*index=5*/s32[]{:T(128)}) while((s32[]{:T(128)}, f32[3,64]{1,0:T(4,128)S(1)}, f32[16,3,2048]{2,0,1:T(8,128)S(1)}, s32[16,2048]{1,0:T(8,128)S(1)}, s32[]{:T(128)}, /*index=5*/s32[]{:T(128)}) %tuple.46), condition=%wide.region_5.6_spmd.clone, body=%wide.region_4.5_spmd.clone.sunk | while | flops 4850051 | bytes 99927 | solution.py:104
  184.8 73.9 %psum.7 = f32[32]{0:T(128)} all-reduce(f32[32]{0:T(128)S(1)} %convolution_bitcast_fusion.1), channel_id=1, replica_groups=mesh['stream'=8,'span'=16,'vert'=4] {'stream','vert'}, use_global_device_ids=true, to_apply=%region_6.7 | all-reduce | flops 32 | bytes 256 | tf_op jit(solution)/shard_map/psum | solution.py:167
  (145 shorter events, 32.0 us)
Async XLA Ops:
  0.6 184.1 %copy-start = (f32[3,64,32]{1,2,0:T(8,128)S(1)}, f32[3,64,32]{1,2,0:T(8,128)}, u32[]{:S(2)}) copy-start(f32[3,64,32]{1,2,0:T(8,128)} %param.20) | copy-start | bytes 73732
  2.8 7.1 %copy-start.14 = (s32[64,1]{0,1:T(1,128)S(1)}, s32[64,1]{0,1:T(1,128)}, u32[]{:S(2)}) copy-start(s32[64,1]{0,1:T(1,128)} %param.16) | copy-start | bytes 772
  2.8 7.4 %copy-start.11 = (f32[64,5,256]{2,0,1:T(8,128)S(1)}, f32[64,5,256]{2,0,1:T(8,128)}, u32[]{:S(2)}) copy-start(f32[64,5,256]{2,0,1:T(8,128)} %param.15) | copy-start | bytes 983044
  3.4 25.8 %collective-permute-start = (f32[5,32,16,1]{1,2,3,0:T(8,128)S(1)}, f32[5,32,16,1]{1,2,3,0:T(8,128)S(1)}, u32[]{:S(2)}, u32[]{:S(2)}) collective-permute-start(f32[5,32,16,1]{1,2,3,0:T(8,128)S(1)} %copy.55), channel_id=1, source_target_pairs={{64,0},{128,64},{192,128},{256,192},{320,256},{384,320},{448,384},... | collective-permute-start | bytes 30728 | tf_op jit(solution)/shard_map/ppermute | solution.py:27
  6.4 23.5 %collective-permute-start.1 = (f32[5,32,16,1]{1,2,3,0:T(8,128)S(1)}, f32[5,32,16,1]{1,2,3,0:T(8,128)S(1)}, u32[]{:S(2)}, u32[]{:S(2)}) collective-permute-start(f32[5,32,16,1]{1,2,3,0:T(8,128)S(1)} %copy.56), channel_id=1, source_target_pairs={{0,64},{64,128},{128,192},{192,256},{256,320},{320,384},{384,448},... | collective-permute-start | bytes 30728 | tf_op jit(solution)/shard_map/ppermute | solution.py:24
  10.7 15.7 %copy-start.1 = (f32[5,32,16,128]{3,2,1,0:T(8,128)S(1)}, f32[5,32,16,128]{3,2,1,0:T(8,128)}, u32[]{:S(2)}) copy-start(f32[5,32,16,128]{3,2,1,0:T(8,128)} %param.13) | copy-start | bytes 3932164
  12.2 15.1 %copy-start.13 = (s32[1,1,1,2048]{3,2,1,0:T(1,128)S(1)}, s32[1,1,1,2048]{3,2,1,0:T(1,128)}, u32[]{:S(2)}) copy-start(s32[1,1,1,2048]{3,2,1,0:T(1,128)} %param.17) | copy-start | bytes 24580
  12.2 42.6 %all-to-all-start = ((f32[64,1,2560]{2,1,0:T(1,128)}), f32[64,1,2560]{2,1,0:T(1,128)}, u32[]{:S(2)}, u32[]{:S(2)}) async-start(f32[64,1,2560]{2,1,0:T(1,128)} %all_to_all.8), calls=%async_computation | async-start | bytes 1310720 | tf_op jit(solution)/shard_map/all_to_all | solution.py:128
  29.9 17.9 %copy-start.2 = (f32[5,32,16,1]{3,2,1,0:T(8,128)}, f32[5,32,16,1]{3,2,1,0:T(8,128)S(1)}, u32[]{:S(2)}) copy-start(f32[5,32,16,1]{3,2,1,0:T(8,128)S(1)} %copy.37) | copy-start | bytes 30724
  31.6 7.8 %copy-start.3 = (f32[5,32,16,1]{3,2,1,0:T(8,128)S(1)}, f32[5,32,16,1]{3,2,1,0:T(8,128)}, u32[]{:S(2)}) copy-start(f32[5,32,16,1]{3,2,1,0:T(8,128)} %copy.39) | copy-start | bytes 30724
  34.0 4.4 %collective-permute-start.2 = (f32[5,32,1,130]{3,2,1,0:T(1,128)S(1)}, f32[5,32,1,130]{3,2,1,0:T(1,128)S(1)}, u32[]{:S(2)}, u32[]{:S(2)}) collective-permute-start(f32[5,32,1,130]{3,2,1,0:T(1,128)S(1)} %get-tuple-element.80), channel_id=1, source_target_pairs={{4,0},{8,4},{12,8},{16,12},{20,16},{24,20},{28,24},{32,28},{36,32}... | collective-permute-start | bytes 249608 | tf_op jit(solution)/shard_map/ppermute | solution.py:27
  35.3 4.0 %collective-permute-start.3 = (f32[5,32,1,130]{3,2,1,0:T(1,128)S(1)}, f32[5,32,1,130]{3,2,1,0:T(1,128)S(1)}, u32[]{:S(2)}, u32[]{:S(2)}) collective-permute-start(f32[5,32,1,130]{3,2,1,0:T(1,128)S(1)} %get-tuple-element.79), channel_id=1, source_target_pairs={{0,4},{4,8},{8,12},{12,16},{16,20},{20,24},{24,28},{28,32},{32,36}... | collective-permute-start | bytes 249608 | tf_op jit(solution)/shard_map/ppermute | solution.py:24
  39.5 7.2 %collective-permute-start.4 = (f32[5,1,18,130]{3,2,1,0:T(8,128)S(1)}, f32[5,1,18,130]{3,2,1,0:T(8,128)S(1)}, u32[]{:S(2)}, u32[]{:S(2)}) collective-permute-start(f32[5,1,18,130]{3,2,1,0:T(8,128)S(1)} %get-tuple-element.72), channel_id=1, source_target_pairs={{1,0},{2,1},{3,2},{5,4},{6,5},{7,6},{9,8},{10,9},{11,10},{13,12},{... | collective-permute-start | bytes 140408 | tf_op jit(solution)/shard_map/ppermute | solution.py:27
  40.9 7.0 %collective-permute-start.5 = (f32[5,1,18,130]{3,2,1,0:T(8,128)S(1)}, f32[5,1,18,130]{3,2,1,0:T(8,128)S(1)}, u32[]{:S(2)}, u32[]{:S(2)}) collective-permute-start(f32[5,1,18,130]{3,2,1,0:T(8,128)S(1)} %get-tuple-element.71), channel_id=1, source_target_pairs={{0,1},{1,2},{2,3},{4,5},{5,6},{6,7},{8,9},{9,10},{10,11},{12,13},{... | collective-permute-start | bytes 140408 | tf_op jit(solution)/shard_map/ppermute | solution.py:24
  46.7 4.3 %copy-start.6 = (f32[32,16,128]{2,1,0:T(8,128)S(1)}, f32[32,16,128]{2,1,0:T(8,128)}, u32[]{:S(2)}) copy-start(f32[32,16,128]{2,1,0:T(8,128)} %param.14) | copy-start | bytes 786436
  46.7 4.3 %copy-start.8 = (f32[5,1,18,130]{3,2,1,0:T(8,128)}, f32[5,1,18,130]{3,2,1,0:T(8,128)S(1)}, u32[]{:S(2)}) copy-start(f32[5,1,18,130]{3,2,1,0:T(8,128)S(1)} %collective-permute-done.4) | copy-start | bytes 140404
  47.8 3.2 %copy-start.9 = (f32[5,1,18,130]{3,2,1,0:T(8,128)}, f32[5,1,18,130]{3,2,1,0:T(8,128)S(1)}, u32[]{:S(2)}) copy-start(f32[5,1,18,130]{3,2,1,0:T(8,128)S(1)} %collective-permute-done.5) | copy-start | bytes 140404
  57.4 26.4 %copy-start.16 = (f32[5]{0:T(128)S(1)}, f32[5]{0:T(128)}, u32[]{:S(2)}) copy-start(f32[5]{0:T(128)} %constant.116.clone) | copy-start | bytes 64
  57.5 26.5 %copy-start.15 = (f32[5]{0:T(128)S(1)}, f32[5]{0:T(128)}, u32[]{:S(2)}) copy-start(f32[5]{0:T(128)} %constant.117.clone) | copy-start | bytes 64
  93.4 9.7 %copy-start.12 = (s32[1,16,1,2048]{3,2,1,0:T(1,128)S(1)}, s32[1,16,1,2048]{3,2,1,0:T(1,128)}, u32[]{:S(2)}) copy-start(s32[1,16,1,2048]{3,2,1,0:T(1,128)} %param.19) | copy-start | bytes 393220
  95.3 7.8 %collective-permute-start.6 = (f32[5,32,16,1]{1,2,3,0:T(8,128)S(1)}, f32[5,32,16,1]{1,2,3,0:T(8,128)S(1)}, u32[]{:S(2)}, u32[]{:S(2)}) collective-permute-start(f32[5,32,16,1]{1,2,3,0:T(8,128)S(1)} %copy.44), channel_id=1, source_target_pairs={{64,0},{128,64},{192,128},{256,192},{320,256},{384,320},{448,384},... | collective-permute-start | bytes 30728 | tf_op jit(solution)/shard_map/ppermute | solution.py:27
  100.8 7.1 %collective-permute-start.7 = (f32[5,32,16,1]{1,2,3,0:T(8,128)S(1)}, f32[5,32,16,1]{1,2,3,0:T(8,128)S(1)}, u32[]{:S(2)}, u32[]{:S(2)}) collective-permute-start(f32[5,32,16,1]{1,2,3,0:T(8,128)S(1)} %copy.46), channel_id=1, source_target_pairs={{0,64},{64,128},{128,192},{192,256},{256,320},{320,384},{384,448},... | collective-permute-start | bytes 30728 | tf_op jit(solution)/shard_map/ppermute | solution.py:24
  109.5 8.4 %copy-start.5 = (f32[5,32,16,1]{3,2,1,0:T(8,128)S(1)}, f32[5,32,16,1]{3,2,1,0:T(8,128)}, u32[]{:S(2)}) copy-start(f32[5,32,16,1]{3,2,1,0:T(8,128)} %copy.47) | copy-start | bytes 30724
  112.3 5.5 %copy-start.4 = (f32[5,32,16,1]{3,2,1,0:T(8,128)S(1)}, f32[5,32,16,1]{3,2,1,0:T(8,128)}, u32[]{:S(2)}) copy-start(f32[5,32,16,1]{3,2,1,0:T(8,128)} %copy.45) | copy-start | bytes 30724
  112.4 4.5 %collective-permute-start.8 = (f32[5,32,1,130]{3,2,1,0:T(1,128)S(1)}, f32[5,32,1,130]{3,2,1,0:T(1,128)S(1)}, u32[]{:S(2)}, u32[]{:S(2)}) collective-permute-start(f32[5,32,1,130]{3,2,1,0:T(1,128)S(1)} %get-tuple-element.76), channel_id=1, source_target_pairs={{4,0},{8,4},{12,8},{16,12},{20,16},{24,20},{28,24},{32,28},{36,32}... | collective-permute-start | bytes 249608 | tf_op jit(solution)/shard_map/ppermute | solution.py:27
  113.8 4.0 %collective-permute-start.9 = (f32[5,32,1,130]{3,2,1,0:T(1,128)S(1)}, f32[5,32,1,130]{3,2,1,0:T(1,128)S(1)}, u32[]{:S(2)}, u32[]{:S(2)}) collective-permute-start(f32[5,32,1,130]{3,2,1,0:T(1,128)S(1)} %get-tuple-element.75), channel_id=1, source_target_pairs={{0,4},{4,8},{8,12},{12,16},{16,20},{20,24},{24,28},{28,32},{32,36}... | collective-permute-start | bytes 249608 | tf_op jit(solution)/shard_map/ppermute | solution.py:24
  118.0 7.5 %collective-permute-start.10 = (f32[5,1,18,130]{3,2,1,0:T(8,128)S(1)}, f32[5,1,18,130]{3,2,1,0:T(8,128)S(1)}, u32[]{:S(2)}, u32[]{:S(2)}) collective-permute-start(f32[5,1,18,130]{3,2,1,0:T(8,128)S(1)} %get-tuple-element.70), channel_id=1, source_target_pairs={{1,0},{2,1},{3,2},{5,4},{6,5},{7,6},{9,8},{10,9},{11,10},{13,12},{... | collective-permute-start | bytes 140408 | tf_op jit(solution)/shard_map/ppermute | solution.py:27
  119.5 7.4 %collective-permute-start.11 = (f32[5,1,18,130]{3,2,1,0:T(8,128)S(1)}, f32[5,1,18,130]{3,2,1,0:T(8,128)S(1)}, u32[]{:S(2)}, u32[]{:S(2)}) collective-permute-start(f32[5,1,18,130]{3,2,1,0:T(8,128)S(1)} %get-tuple-element.69), channel_id=1, source_target_pairs={{0,1},{1,2},{2,3},{4,5},{5,6},{6,7},{8,9},{9,10},{10,11},{12,13},{... | collective-permute-start | bytes 140408 | tf_op jit(solution)/shard_map/ppermute | solution.py:24
  135.3 1.1 copy-start.7
  136.4 37.5 %copy-start.10 = (f32[1,16,1,3,2048]{4,2,3,1,0:T(1,128)S(1)}, f32[1,16,1,3,2048]{4,2,3,1,0:T(1,128)}, u32[]{:S(2)}) copy-start(f32[1,16,1,3,2048]{4,2,3,1,0:T(1,128)} %param.18) | copy-start | bytes 1179652
